TPU v7x, 32 devices: a whole 2x2x4 slice. The times are simulated.
32 devices in a mesh: group: 2 (over x), dp: 16 (over z, y, core).
Axes of the slice: x: 2, y: 2, z: 4, core: 2. Of those that a mesh axis runs over, the one named last changes fastest.
Arguments:
- candidate_queries: bfloat16 [256, 8, 16, 4096], P(('group', 'dp')), parts along dimension 0, may hold values from -10 to 10
- target_states: bfloat16 [256, 32, 1024], P(('group', 'dp')), parts along dimension 0, may hold values from -4 to 4
- target_queries: bfloat16 [256, 32, 4096], P(('group', 'dp')), parts along dimension 0, may hold values from -10 to 10
- candidate_states: bfloat16 [2048, 16, 1024], P(('group', 'dp')), parts along dimension 0, may hold values from -4 to 4
- target_length: int32 [256], P(('group', 'dp')), parts along dimension 0, may hold values from 2 to 32
- candidate_length: int32 [256, 8], P(('group', 'dp')), parts along dimension 0, may hold values from 2 to 16
- candidate_row: int32 [256, 8], P(('group', 'dp')), parts along dimension 0, may hold values from 0 to 63, as said below
- direct_readout: bfloat16 [4096], replicated, may hold values from -0.5 to 0.5
- channel_readout: bfloat16 [4096], replicated, may hold values from -0.5 to 0.5
Outputs:
- rescored: float32 [2048], P(('group', 'dp')), parts along dimension 0
There are 2 independent parts, one for each index of `group`. A program takes and returns all parts, laid end to end along the dimension named above; an argument that names none is the same for every part. Nothing has to cross between parts.
Inputs may be any that keep to these rules, and one draw needn't show every extreme that they name: `candidate_row`: on the 8 targets of each aligned block (targets b * 8 to (b + 1) * 8 - 1), the 64 entries hold every value from 0 to 63 once.
All inputs are finite; a program needn't handle non-finite values.
Results may differ from a plain program's by a relative error of at most 0.0021.
Values may be sent and summed in bfloat16 or wider, within the bound.
A program may use at most 128 MiB of HBM per device.

v0:
```python
import functools
import math

import jax
import jax.numpy as jnp
from jax import lax
from jax.experimental import pallas as pl
from jax.experimental.pallas import tpu as pltpu
from jax.sharding import PartitionSpec as P

HEAD_SIZE = 128
AXIS = "dp"
MESH = pl.DeviceIdType.MESH
EARLY = 3
masked_score = -1e30


def dot_nt(a, b):
    return lax.dot_general(
        a, b, (((1,), (1,)), ((), ())), preferred_element_type=jnp.float32
    )


def exchange(a, b, n):
    if n & (n - 1):
        return lax.rem(a + b, n)
    out, bit = 0, 1
    while bit < n:
        out = out + lax.rem(a // bit + b // bit, 2) * bit
        bit *= 2
    return out


def turn(i, n):
    return lax.select(
        lax.rem(i, 2) == 0, n - 1 - i // 2, lax.max(n // 2 - 1 - i // 2, 1)
    ) if n % 2 == 0 and n > 2 else n - 1 - i


def expect(a, b, n):
    if n & (n - 1):
        return lax.rem(a + n - b, n)
    return exchange(a, b, n)


def ratio(scores, values, keys_left):
    keys = lax.broadcasted_iota(jnp.int32, scores.shape, 0)
    scores = jnp.where(keys < keys_left, scores, masked_score)
    highest = jnp.max(scores, axis=0, keepdims=True)
    factor = math.log2(math.e) / math.sqrt(HEAD_SIZE)
    weights = jnp.exp2((scores - highest) * factor)
    return jnp.sum(weights * values, axis=0, keepdims=True) / jnp.sum(
        weights, axis=0, keepdims=True
    )


def kernel(
    n, dims,
    stored_in, sources_in, lengths_in, direct_in, channel_in, cq, ts, tq, cs,
    out,
    stored, sources, lengths, direct_r, channel_r,
    cq_buf, ts_buf, tq_buf, v_buf, k_buf, u_out, u_buf, spread, ud, rd, sel, dsum, r_out, r_buf,
    in_sem, cq_sem, ks, kr, us, ur, rs, rr,
):
    T, S, I, J, H, G = dims
    C = T * S
    rpp = C // n
    hg = H // G
    D = HEAD_SIZE
    me = lax.axis_index(AXIS)

    loads = [
        pltpu.make_async_copy(cs.at[:, :, :, pl.ds(G * D, G * D)], v_buf, in_sem.at[0]),
        pltpu.make_async_copy(
            cs.at[me, :, :, pl.ds(0, G * D)], k_buf.at[me], in_sem.at[1]
        ),
        pltpu.make_async_copy(ts, ts_buf, in_sem.at[2]),
        pltpu.make_async_copy(tq, tq_buf, in_sem.at[3]),
        pltpu.make_async_copy(channel_in, channel_r, in_sem.at[4]),
        pltpu.make_async_copy(direct_in, direct_r, in_sem.at[5]),
        pltpu.make_async_copy(stored_in, stored, in_sem.at[6]),
        pltpu.make_async_copy(sources_in, sources, in_sem.at[7]),
        pltpu.make_async_copy(lengths_in, lengths, in_sem.at[8]),
    ]
    def cq_copy(t):
        return pltpu.make_async_copy(cq.at[t], cq_buf.at[t], cq_sem.at[t])

    barrier = pltpu.get_barrier_semaphore()

    def greet(k, carry):
        pl.semaphore_signal(
            barrier, inc=1, device_id={AXIS: exchange(me, k, n)}, device_id_type=MESH
        )
        return carry

    lax.fori_loop(1, n, greet, 0)
    for load in loads[4:]:
        load.start()
    loads[0].start()
    loads[2].start()
    cq_copy(0).start()

    def k_copy(p, slot):
        return pltpu.make_async_remote_copy(
            src_ref=cs.at[p, :, :, pl.ds(0, G * D)],
            dst_ref=k_buf.at[slot], send_sem=ks.at[p], recv_sem=kr.at[slot],
            device_id={AXIS: p}, device_id_type=MESH,
        )

    def u_copy(p, slot):
        return pltpu.make_async_remote_copy(
            src_ref=u_out.at[p], dst_ref=u_buf.at[slot], send_sem=us.at[p],
            recv_sem=ur.at[slot], device_id={AXIS: p}, device_id_type=MESH,
        )

    def r_copy(p, slot):
        return pltpu.make_async_remote_copy(
            src_ref=r_out.at[p], dst_ref=r_buf.at[slot], send_sem=rs.at[p],
            recv_sem=rr.at[slot], device_id={AXIS: p}, device_id_type=MESH,
        )

    def k_send(i, carry):
        p = exchange(me, turn(i, n), n)
        k_copy(p, me).start()
        return carry

    pl.semaphore_wait(barrier, n - 1)
    early = min(EARLY, n - 1)
    lax.fori_loop(0, early, k_send, 0)
    loads[1].start()
    for t in range(1, T):
        cq_copy(t).start()
    loads[3].start()

    wide = u_out.shape[2]
    head_id = lax.broadcasted_iota(jnp.int32, (H, D), 0)
    rows_r = jnp.zeros((H, D), jnp.float32)
    loads[4].wait()
    for h in range(H):
        row = channel_r[h * D : (h + 1) * D].astype(jnp.float32).reshape(1, D)
        rows_r = jnp.where(head_id == h, row, rows_r)
    rows_r = jnp.concatenate([rows_r.astype(jnp.bfloat16)] * (wide // H), axis=0)
    row_id = lax.broadcasted_iota(jnp.int32, (wide, D), 0)
    loads[0].wait()
    u = None
    for r in range(rpp):
        for g in range(G):
            weights = jnp.where(
                row_id // hg == r * G + g, rows_r, jnp.zeros_like(rows_r)
            )
            values = v_buf[:, r, :, g * D : (g + 1) * D]
            values = values.reshape(n * I, D)
            part = dot_nt(values, weights)
            u = part if u is None else u + part
    u_out[...] = u.reshape(n, I, wide)

    lane = lax.broadcasted_iota(jnp.int32, (wide, hg * J), 1)
    head = lax.broadcasted_iota(jnp.int32, (wide, hg * J), 0)
    for r in range(rpp):
        for g in range(G):
            hit = head == lane // J + (r * H + g * hg)
            sel[r * G + g] = jnp.where(hit, 1.0, 0.0).astype(jnp.bfloat16)

    def u_send(i, carry):
        u_copy(exchange(me, turn(i, n), n), me).start()
        return carry

    lax.fori_loop(0, n - 1, u_send, 0)
    lax.fori_loop(early, n - 1, k_send, 0)

    rows = S * I
    slot = lax.broadcasted_iota(jnp.int32, (1, rows), 1) // I
    for load in loads[5:]:
        load.wait()
    for t in range(T):
        held = jnp.zeros((1, rows), jnp.int32)
        count = jnp.zeros((1, rows), jnp.int32)
        for c in range(S):
            held = jnp.where(slot == c, stored[t, c], held)
            count = jnp.where(slot == c, sources[t, c], count)
        spread[0, t] = held
        spread[1, t] = count
        spread[2, t] = (count * (J + 1) + lengths[t]) * T + t

    loads[2].wait()
    for g in range(G):
        states = ts_buf[:, :, (G + g) * D : (G + g + 1) * D].reshape(T * J, D)
        for q in range(hg):
            h = g * hg + q
            rd[q * rows : (q + 1) * rows, :] = jnp.broadcast_to(
                direct_r[h * D : (h + 1) * D].astype(jnp.float32).reshape(1, D), (rows, D)
            ).astype(jnp.bfloat16)
        ud[g] = dot_nt(states, rd[...])

    token = lax.rem(lax.broadcasted_iota(jnp.int32, (1, rows), 1), I)

    def direct(t, carry):
        cq_copy(t).wait()
        total = jnp.zeros((1, hg * rows), jnp.float32)
        for g in range(G):
            queries = jnp.concatenate(
                [
                    cq_buf[t, :, (g * hg + q) * D : (g * hg + q + 1) * D]
                    for q in range(hg)
                ],
                axis=0,
            )
            scores = dot_nt(ts_buf[t, :, g * D : (g + 1) * D], queries)
            values = ud[g, pl.ds(pl.multiple_of(t * J, J), J), :]
            total = total + ratio(scores, values, lengths[t])
        tokens = total[:, 0:rows]
        for q in range(1, hg):
            tokens = tokens + total[:, q * rows : (q + 1) * rows]
        count = spread[1, t]
        dsum[t] = jnp.where(token < count, tokens, 0.0) / count.astype(jnp.float32)
        return carry

    lax.fori_loop(0, T, direct, 0)

    loads[3].wait()
    lanes = out.shape[1]
    place = lax.broadcasted_iota(jnp.int32, (1, lanes), 1)
    position = lax.rem(lax.broadcasted_iota(jnp.int32, (1, hg * J), 1), J)
    direct_sums = dsum[...]
    owners = spread[0]
    codes = spread[2]

    def lookup(p):
        return [
            jnp.max(jnp.where(owners == p * rpp + r, codes, 0)) for r in range(rpp)
        ]

    def block(p, found):
        result = jnp.zeros((1, lanes), jnp.float32)
        whole = u_buf[p]
        high = whole.astype(jnp.bfloat16)
        low = (whole - high.astype(jnp.float32)).astype(jnp.bfloat16)
        sent = jnp.concatenate([high, low], axis=0)
        for r in range(rpp):
            v = p * rpp + r
            t = lax.rem(found[r], T)
            target_count = lax.rem(found[r] // T, J + 1)
            source_count = found[r] // (T * (J + 1))
            total = jnp.zeros((1, hg * J), jnp.float32)
            for g in range(G):
                queries = jnp.concatenate(
                    [
                        tq_buf[t, :, (g * hg + q) * D : (g * hg + q + 1) * D]
                        for q in range(hg)
                    ],
                    axis=0,
                )
                scores = dot_nt(k_buf[p, r, :, g * D : (g + 1) * D], queries)
                values = jnp.dot(
                    sent, sel[r * G + g], preferred_element_type=jnp.float32
                )
                values = values[:I] + values[I:]
                total = total + ratio(scores, values, source_count)
            kept = jnp.where(position < target_count, total, 0.0)
            channel = jnp.sum(kept, axis=1, keepdims=True)
            channel = channel / target_count.astype(jnp.float32)
            own = jnp.where(owners == v, direct_sums, 0.0)
            own = jnp.sum(jnp.sum(own, axis=0), axis=1, keepdims=True)
            result = result + jnp.where(place == me * rpp + r, own + channel, 0.0)
        return jnp.broadcast_to(result, (8, lanes))

    u_buf[me] = u_out[me]
    loads[1].wait()
    r_buf[me] = block(me, lookup(me))

    def channel_step(i, carry):
        p = expect(me, turn(i, n), n)
        found = lookup(p)
        k_copy(p, p).wait_recv()
        u_copy(p, p).wait_recv()
        r_out[p] = block(p, found)
        r_copy(p, me).start()
        return carry

    lax.fori_loop(0, n - 1, channel_step, 0)

    def finish(i, carry):
        p = expect(me, turn(i, n), n)
        r_copy(p, p).wait_recv()
        k_copy(p, p).wait_send()
        u_copy(p, p).wait_send()
        r_copy(p, p).wait_send()
        return carry

    lax.fori_loop(0, n - 1, finish, 0)
    out[...] = jnp.sum(r_buf[...], axis=0)


def on_device(
    n,
    candidate_queries,
    target_states,
    target_queries,
    candidate_states,
    target_length,
    candidate_length,
    candidate_row,
    direct_readout,
    channel_readout,
):
    T, S, I, QW = candidate_queries.shape
    J = target_states.shape[1]
    H = QW // HEAD_SIZE
    G = target_states.shape[2] // (2 * HEAD_SIZE)
    C = T * S
    rpp = C // n
    hg = H // G
    wide = max(128, rpp * H)
    lanes = -(-C // 128) * 128
    bf, f32 = jnp.bfloat16, jnp.float32
    vmem, smem = pltpu.VMEM, pltpu.SMEM
    anywhere = pl.BlockSpec(memory_space=pl.ANY)
    dma = pltpu.SemaphoreType.DMA
    found = pl.pallas_call(
        functools.partial(kernel, n, (T, S, I, J, H, G)),
        out_shape=jax.ShapeDtypeStruct((8, lanes), f32),
        in_specs=[
            anywhere, anywhere, anywhere, anywhere, anywhere,
            anywhere, anywhere, anywhere, anywhere,
        ],
        out_specs=pl.BlockSpec(memory_space=vmem),
        scratch_shapes=[
            smem((T, S), jnp.int32),
            smem((T, S), jnp.int32),
            smem((T,), jnp.int32),
            vmem((QW,), bf),
            vmem((QW,), bf),
            vmem((T, S * I, QW), bf),
            vmem(target_states.shape, bf),
            vmem(target_queries.shape, bf),
            vmem((n, rpp, I, G * HEAD_SIZE), bf),
            vmem((n, rpp, I, G * HEAD_SIZE), bf),
            vmem((n, I, wide), f32),
            vmem((n, I, wide), f32),
            vmem((3, T, 1, S * I), jnp.int32),
            vmem((G, T * J, hg * S * I), f32),
            vmem((hg * S * I, HEAD_SIZE), bf),
            vmem((rpp * G, wide, hg * J), bf),
            vmem((T, 1, S * I), f32),
            vmem((n, 8, lanes), f32),
            vmem((n, 8, lanes), f32),
            dma((9,)), dma((T,)),
            dma((n,)), dma((n,)), dma((n,)), dma((n,)), dma((n,)), dma((n,)),
        ],
        compiler_params=pltpu.CompilerParams(
            collective_id=0, has_side_effects=True, vmem_limit_bytes=60 << 20
        ),
    )(
        candidate_row, candidate_length, target_length,
        direct_readout, channel_readout,
        candidate_queries.reshape(T, S * I, QW),
        target_states, target_queries,
        candidate_states.reshape(n, rpp, I, 2 * G * HEAD_SIZE),
    )
    return found[0, :C]


def solution(mesh):
    in_specs = (
        P(("group", "dp"), None, None, None),
        P(("group", "dp"), None, None),
        P(("group", "dp"), None, None),
        P(("group", "dp"), None, None),
        P(("group", "dp")),
        P(("group", "dp"), None),
        P(("group", "dp"), None),
        P(),
        P(),
    )
    return jax.shard_map(
        functools.partial(on_device, mesh.shape[AXIS]),
        mesh=mesh, in_specs=in_specs, out_specs=P(("group", "dp")), check_vma=False,
    )
```

profile of v0, /device:TPU:0, one launch (start us, length us, event | category | flops | bytes accessed | tf_op | source)
XLA Modules:
  0.0 42.0 jit_solution(17681010426823943460)
XLA Ops:
  0.0 40.8 %shard_map.91 = f32[8,128]{1,0:T(8,128)} custom-call(s32[8,8]{1,0:T(8,128)} %stored_in.1, s32[8,8]{1,0:T(8,128)} %sources_in.1, s32[8]{0:T(128)} %lengths_in.1, bf16[4096]{0:T(1024)(128)(2,1)} %direct_in.1, bf16[4096]{0:T(1024)(128)(2,1)} %channel_in.1, bf16[8,128,4096]{2,1,0:T(8,128)(2,1)} %bitcast.4, bf16[8,32,1024]{2,1,0:T(8,128)(2,1)} %ts.1, ...), custom_call_target="tpu_custom_call" | custom-call | tf_op jit(solution)/shard_map/pallas_call | solution.py:319
  40.8 1.2 %slice_bitcast_fusion = f32[64]{0:T(128)} fusion(f32[8,128]{1,0:T(8,128)} %shard_map.91), kind=kLoop, calls=%fused_computation | loop fusion | bytes 512 | tf_op jit(solution)/shard_map/squeeze | solution.py:360
where the time goes:
time: 42.2 us; the launch traced here: 42 us
  Pallas kernels  40.8 us (97%)
  local copies, waits for them, and re-layouts  1.19 us (3%)
    pallas_call x1, Pallas kernels, on_device(): pl.pallas_call(functools.partial(kernel, n, (T, S, I, J, H, G)), out_shap...  40.8 us
    squeeze x1, local copies, waits for them, and re-layouts, on_device(): return found[0, :C]  1.19 us

commit v1 on v0

--- a/solution.py
+++ b/solution.py
@@ -11,7 +11,7 @@
 HEAD_SIZE = 128
 AXIS = "dp"
 MESH = pl.DeviceIdType.MESH
-EARLY = 3
+EARLY = 2
 masked_score = -1e30
 
 
@@ -21,26 +21,46 @@
     )
 
 
-def exchange(a, b, n):
-    if n & (n - 1):
-        return lax.rem(a + b, n)
-    out, bit = 0, 1
-    while bit < n:
-        out = out + lax.rem(a // bit + b // bit, 2) * bit
-        bit *= 2
-    return out
-
-
-def turn(i, n):
-    return lax.select(
-        lax.rem(i, 2) == 0, n - 1 - i // 2, lax.max(n // 2 - 1 - i // 2, 1)
-    ) if n % 2 == 0 and n > 2 else n - 1 - i
-
-
-def expect(a, b, n):
-    if n & (n - 1):
-        return lax.rem(a + n - b, n)
-    return exchange(a, b, n)
+class Peers:
+    def __init__(self, me, n):
+        assert n >= 4 and n & (n - 1) == 0
+        m = n // 4
+        self.me, self.n, self.m = me, n, m
+        self.quarter = lax.div(me, m)
+        low = 1 - 2 * lax.rem(self.quarter, 2)
+        high = 1 - 2 * lax.div(self.quarter, 2)
+        self.outer = lax.rem(self.quarter + lax.div(self.quarter, 2), 2) == 0
+        one, two = low * m, high * (2 * m)
+        self.one, self.two, self.three = me + one, me + two, me + one + two
+        self.far = lax.select(self.outer, self.three, self.two)
+        self.near = lax.select(self.outer, self.two, self.three)
+        steps, bit = [0], 1
+        while bit < m:
+            step = (1 - 2 * lax.rem(lax.div(me, bit), 2)) * bit
+            steps = steps + [s + step for s in steps]
+            bit *= 2
+        self.steps = steps
+
+    def inside(self):
+        return [self.me + s for s in self.steps[1:]]
+
+    def at(self, base):
+        return [base + s for s in self.steps]
+
+    def arrival(self, i):
+        m = self.m
+        late = i - (2 * m - 1)
+        j = lax.select(i < m - 1, i + 1, lax.select(late < 0, i - (m - 1), lax.div(late, 2)))
+        base = lax.select(
+            i < m - 1, self.me,
+            lax.select(late < 0, self.far, lax.select(lax.rem(late, 2) == 0, self.one, self.near)),
+        )
+        peer, bit = base, 1
+        while bit < m:
+            step = (1 - 2 * lax.rem(lax.div(self.me, bit), 2)) * bit
+            peer = peer + step * lax.rem(lax.div(j, bit), 2)
+            bit *= 2
+        return peer
 
 
 def ratio(scores, values, keys_left):
@@ -60,7 +80,7 @@
     out,
     stored, sources, lengths, direct_r, channel_r,
     cq_buf, ts_buf, tq_buf, v_buf, k_buf, u_out, u_buf, spread, ud, rd, sel, dsum, r_out, r_buf,
-    in_sem, cq_sem, ks, kr, us, ur, rs, rr,
+    in_sem, cq_sem, ks, kr, us, ur, rs, rr, ready,
 ):
     T, S, I, J, H, G = dims
     C = T * S
@@ -86,14 +106,23 @@
         return pltpu.make_async_copy(cq.at[t], cq_buf.at[t], cq_sem.at[t])
 
     barrier = pltpu.get_barrier_semaphore()
-
-    def greet(k, carry):
+    peers = Peers(me, n)
+    m = n // 4
+    last = peers.quarter == 3
+
+    def say(peer, semaphore):
         pl.semaphore_signal(
-            barrier, inc=1, device_id={AXIS: exchange(me, k, n)}, device_id_type=MESH
+            semaphore, inc=1, device_id={AXIS: peer}, device_id_type=MESH
         )
-        return carry
-
-    lax.fori_loop(1, n, greet, 0)
+
+    for peer in peers.inside():
+        say(peer, barrier)
+    cross = peers.at(peers.two) + peers.at(peers.three)
+    for peer in cross + peers.at(peers.one):
+        @pl.when(jnp.logical_or(jnp.logical_not(last), lax.div(peer, m) == 3))
+        def _(peer=peer):
+            say(peer, barrier)
+
     for load in loads[4:]:
         load.start()
     loads[0].start()
@@ -119,14 +148,23 @@
             recv_sem=rr.at[slot], device_id={AXIS: p}, device_id_type=MESH,
         )
 
-    def k_send(i, carry):
-        p = exchange(me, turn(i, n), n)
-        k_copy(p, me).start()
-        return carry
-
-    pl.semaphore_wait(barrier, n - 1)
-    early = min(EARLY, n - 1)
-    lax.fori_loop(0, early, k_send, 0)
+    @pl.when(last)
+    def _():
+        pl.semaphore_wait(barrier, n - 1)
+        for peer in cross + peers.at(peers.one):
+            say(peer, ready)
+
+    @pl.when(jnp.logical_not(last))
+    def _():
+        pl.semaphore_wait(barrier, n - 1 - m)
+
+    inner = lax.div(peers.quarter, 2) == 0
+    first = lax.select(inner, lax.select(peers.outer, peers.near, peers.near), peers.far)
+    first = peers.at(first)[: min(EARLY, m)]
+    second = peers.at(peers.far)
+    third = peers.at(peers.near)
+    for peer in first:
+        k_copy(peer, me).start()
     loads[1].start()
     for t in range(1, T):
         cq_copy(t).start()
@@ -152,7 +190,7 @@
             values = values.reshape(n * I, D)
             part = dot_nt(values, weights)
             u = part if u is None else u + part
-    u_out[...] = u.reshape(n, I, wide)
+    u_out[...] = u.astype(jnp.bfloat16).reshape(n, I, wide)
 
     lane = lax.broadcasted_iota(jnp.int32, (wide, hg * J), 1)
     head = lax.broadcasted_iota(jnp.int32, (wide, hg * J), 0)
@@ -161,12 +199,29 @@
             hit = head == lane // J + (r * H + g * hg)
             sel[r * G + g] = jnp.where(hit, 1.0, 0.0).astype(jnp.bfloat16)
 
-    def u_send(i, carry):
-        u_copy(exchange(me, turn(i, n), n), me).start()
-        return carry
-
-    lax.fori_loop(0, n - 1, u_send, 0)
-    lax.fori_loop(early, n - 1, k_send, 0)
+    @pl.when(jnp.logical_not(last))
+    def _():
+        pl.semaphore_wait(ready, m)
+
+    for peer in second + third + peers.inside() + peers.at(peers.one):
+        u_copy(peer, me).start()
+    early = len(first)
+    for k, peer in enumerate(second):
+        if k < early:
+            @pl.when(inner)
+            def _(peer=peer):
+                k_copy(peer, me).start()
+        else:
+            k_copy(peer, me).start()
+    for k, peer in enumerate(third):
+        if k < early:
+            @pl.when(jnp.logical_not(inner))
+            def _(peer=peer):
+                k_copy(peer, me).start()
+        else:
+            k_copy(peer, me).start()
+    for peer in peers.inside() + peers.at(peers.one):
+        k_copy(peer, me).start()
 
     rows = S * I
     slot = lax.broadcasted_iota(jnp.int32, (1, rows), 1) // I
@@ -232,10 +287,7 @@
 
     def block(p, found):
         result = jnp.zeros((1, lanes), jnp.float32)
-        whole = u_buf[p]
-        high = whole.astype(jnp.bfloat16)
-        low = (whole - high.astype(jnp.float32)).astype(jnp.bfloat16)
-        sent = jnp.concatenate([high, low], axis=0)
+        sent = u_buf[p]
         for r in range(rpp):
             v = p * rpp + r
             t = lax.rem(found[r], T)
@@ -254,7 +306,6 @@
                 values = jnp.dot(
                     sent, sel[r * G + g], preferred_element_type=jnp.float32
                 )
-                values = values[:I] + values[I:]
                 total = total + ratio(scores, values, source_count)
             kept = jnp.where(position < target_count, total, 0.0)
             channel = jnp.sum(kept, axis=1, keepdims=True)
@@ -262,14 +313,14 @@
             own = jnp.where(owners == v, direct_sums, 0.0)
             own = jnp.sum(jnp.sum(own, axis=0), axis=1, keepdims=True)
             result = result + jnp.where(place == me * rpp + r, own + channel, 0.0)
-        return jnp.broadcast_to(result, (8, lanes))
+        return result
 
     u_buf[me] = u_out[me]
     loads[1].wait()
     r_buf[me] = block(me, lookup(me))
 
     def channel_step(i, carry):
-        p = expect(me, turn(i, n), n)
+        p = peers.arrival(i)
         found = lookup(p)
         k_copy(p, p).wait_recv()
         u_copy(p, p).wait_recv()
@@ -280,7 +331,7 @@
     lax.fori_loop(0, n - 1, channel_step, 0)
 
     def finish(i, carry):
-        p = expect(me, turn(i, n), n)
+        p = peers.arrival(i)
         r_copy(p, p).wait_recv()
         k_copy(p, p).wait_send()
         u_copy(p, p).wait_send()
@@ -318,7 +369,7 @@
     dma = pltpu.SemaphoreType.DMA
     found = pl.pallas_call(
         functools.partial(kernel, n, (T, S, I, J, H, G)),
-        out_shape=jax.ShapeDtypeStruct((8, lanes), f32),
+        out_shape=jax.ShapeDtypeStruct((1, lanes), f32),
         in_specs=[
             anywhere, anywhere, anywhere, anywhere, anywhere,
             anywhere, anywhere, anywhere, anywhere,
@@ -335,17 +386,18 @@
             vmem(target_queries.shape, bf),
             vmem((n, rpp, I, G * HEAD_SIZE), bf),
             vmem((n, rpp, I, G * HEAD_SIZE), bf),
-            vmem((n, I, wide), f32),
-            vmem((n, I, wide), f32),
+            vmem((n, I, wide), bf),
+            vmem((n, I, wide), bf),
             vmem((3, T, 1, S * I), jnp.int32),
             vmem((G, T * J, hg * S * I), f32),
             vmem((hg * S * I, HEAD_SIZE), bf),
             vmem((rpp * G, wide, hg * J), bf),
             vmem((T, 1, S * I), f32),
-            vmem((n, 8, lanes), f32),
-            vmem((n, 8, lanes), f32),
+            vmem((n, 1, lanes), f32),
+            vmem((n, 1, lanes), f32),
             dma((9,)), dma((T,)),
             dma((n,)), dma((n,)), dma((n,)), dma((n,)), dma((n,)), dma((n,)),
+            pltpu.SemaphoreType.REGULAR,
         ],
         compiler_params=pltpu.CompilerParams(
             collective_id=0, has_side_effects=True, vmem_limit_bytes=60 << 20

time: 42.2 us -> 36.8 us (0.87)
  the two profiles are of different devices: /device:TPU:0 before, /device:TPU:1 now
where the time goes in v1:
time: 36.8 us; the launch traced here: 36.6 us
  Pallas kernels  35.4 us (96%)
  local copies, waits for them, and re-layouts  1.19 us (3%)
    pallas_call x1, Pallas kernels, on_device(): pl.pallas_call(functools.partial(kernel, n, (T, S, I, J, H, G)), out_shap...  35.4 us
    squeeze x1, local copies, waits for them, and re-layouts, on_device(): return found[0, :C]  1.19 us

profile of v1, /device:TPU:1, one launch (start us, length us, event | category | flops | bytes accessed | tf_op | source)
XLA Modules:
  0.0 36.6 jit_solution(14536965471652513427)
XLA Ops:
  0.0 35.4 %shard_map.91 = f32[1,128]{1,0:T(1,128)} custom-call(s32[8,8]{1,0:T(8,128)} %stored_in.1, s32[8,8]{1,0:T(8,128)} %sources_in.1, s32[8]{0:T(128)} %lengths_in.1, bf16[4096]{0:T(1024)(128)(2,1)} %direct_in.1, bf16[4096]{0:T(1024)(128)(2,1)} %channel_in.1, bf16[8,128,4096]{2,1,0:T(8,128)(2,1)} %bitcast.4, bf16[8,32,1024]{2,1,0:T(8,128)(2,1)} %ts.1, ...), custom_call_target="tpu_custom_call" | custom-call | tf_op jit(solution)/shard_map/pallas_call | solution.py:370
  35.4 1.2 %slice_bitcast_fusion = f32[64]{0:T(128)} fusion(f32[1,128]{1,0:T(1,128)} %shard_map.91), kind=kLoop, calls=%fused_computation | loop fusion | bytes 512 | tf_op jit(solution)/shard_map/squeeze | solution.py:412

commit v2 on v1

--- a/solution.py
+++ b/solution.py
@@ -12,6 +12,7 @@
 AXIS = "dp"
 MESH = pl.DeviceIdType.MESH
 EARLY = 2
+HELD = 2
 masked_score = -1e30
 
 
@@ -49,12 +50,17 @@
 
     def arrival(self, i):
         m = self.m
-        late = i - (2 * m - 1)
-        j = lax.select(i < m - 1, i + 1, lax.select(late < 0, i - (m - 1), lax.div(late, 2)))
-        base = lax.select(
-            i < m - 1, self.me,
-            lax.select(late < 0, self.far, lax.select(lax.rem(late, 2) == 0, self.one, self.near)),
-        )
+        i = i - (m - 1)
+        early = lax.select(self.outer, 0, min(EARLY, m // 2))
+        late = i - early
+        inside = i < 0
+        near = jnp.logical_or(i < early, i >= 2 * m + early)
+        j = lax.select(i < early, i, i - 2 * m)
+        j = lax.select(near, m - 1 - j, lax.rem(late + m, m))
+        j = lax.select(inside, i + m, j)
+        base = lax.select(late < m, self.far, self.one)
+        base = lax.select(near, self.near, base)
+        base = lax.select(inside, self.me, base)
         peer, bit = base, 1
         while bit < m:
             step = (1 - 2 * lax.rem(lax.div(self.me, bit), 2)) * bit
@@ -78,8 +84,8 @@
     n, dims,
     stored_in, sources_in, lengths_in, direct_in, channel_in, cq, ts, tq, cs,
     out,
-    stored, sources, lengths, direct_r, channel_r,
-    cq_buf, ts_buf, tq_buf, v_buf, k_buf, u_out, u_buf, spread, ud, rd, sel, dsum, r_out, r_buf,
+    stored, sources, lengths, table, direct_r, channel_r,
+    cq_buf, ts_buf, tq_buf, v_buf, k_buf, u_out, u_buf, spread, owners, ud, rd, sel, score, owned, owned_count, dsum, owns, r_out, r_buf,
     in_sem, cq_sem, ks, kr, us, ur, rs, rr, ready,
 ):
     T, S, I, J, H, G = dims
@@ -101,6 +107,8 @@
         pltpu.make_async_copy(stored_in, stored, in_sem.at[6]),
         pltpu.make_async_copy(sources_in, sources, in_sem.at[7]),
         pltpu.make_async_copy(lengths_in, lengths, in_sem.at[8]),
+        pltpu.make_async_copy(stored_in, owned, in_sem.at[9]),
+        pltpu.make_async_copy(sources_in, owned_count, in_sem.at[10]),
     ]
     def cq_copy(t):
         return pltpu.make_async_copy(cq.at[t], cq_buf.at[t], cq_sem.at[t])
@@ -118,9 +126,10 @@
     for peer in peers.inside():
         say(peer, barrier)
     cross = peers.at(peers.two) + peers.at(peers.three)
-    for peer in cross + peers.at(peers.one):
-        @pl.when(jnp.logical_or(jnp.logical_not(last), lax.div(peer, m) == 3))
-        def _(peer=peer):
+
+    @pl.when(jnp.logical_not(last))
+    def _():
+        for peer in cross + peers.at(peers.one):
             say(peer, barrier)
 
     for load in loads[4:]:
@@ -132,20 +141,20 @@
     def k_copy(p, slot):
         return pltpu.make_async_remote_copy(
             src_ref=cs.at[p, :, :, pl.ds(0, G * D)],
-            dst_ref=k_buf.at[slot], send_sem=ks.at[p], recv_sem=kr.at[slot],
+            dst_ref=k_buf.at[slot], send_sem=ks, recv_sem=kr.at[slot],
             device_id={AXIS: p}, device_id_type=MESH,
         )
 
     def u_copy(p, slot):
         return pltpu.make_async_remote_copy(
-            src_ref=u_out.at[p], dst_ref=u_buf.at[slot], send_sem=us.at[p],
+            src_ref=u_out.at[p], dst_ref=u_buf.at[slot], send_sem=us,
             recv_sem=ur.at[slot], device_id={AXIS: p}, device_id_type=MESH,
         )
 
     def r_copy(p, slot):
         return pltpu.make_async_remote_copy(
-            src_ref=r_out.at[p], dst_ref=r_buf.at[slot], send_sem=rs.at[p],
-            recv_sem=rr.at[slot], device_id={AXIS: p}, device_id_type=MESH,
+            src_ref=r_out.at[p], dst_ref=r_buf.at[slot], send_sem=rs,
+            recv_sem=rr, device_id={AXIS: p}, device_id_type=MESH,
         )
 
     @pl.when(last)
@@ -158,12 +167,10 @@
     def _():
         pl.semaphore_wait(barrier, n - 1 - m)
 
-    inner = lax.div(peers.quarter, 2) == 0
-    first = lax.select(inner, lax.select(peers.outer, peers.near, peers.near), peers.far)
-    first = peers.at(first)[: min(EARLY, m)]
-    second = peers.at(peers.far)
-    third = peers.at(peers.near)
-    for peer in first:
+    early = min(EARLY, m // 2)
+    far = peers.at(peers.far)
+    near = peers.at(peers.near)[::-1]
+    for peer in near[:early]:
         k_copy(peer, me).start()
     loads[1].start()
     for t in range(1, T):
@@ -190,37 +197,28 @@
             values = values.reshape(n * I, D)
             part = dot_nt(values, weights)
             u = part if u is None else u + part
+    turn = lax.rem(lax.broadcasted_iota(jnp.int32, u.shape, 1), hg)
+    for q in range(1, hg):
+        error = u - u.astype(jnp.bfloat16).astype(jnp.float32)
+        u = jnp.where(turn == q, u + pltpu.roll(error, 1, 1), u)
     u_out[...] = u.astype(jnp.bfloat16).reshape(n, I, wide)
 
-    lane = lax.broadcasted_iota(jnp.int32, (wide, hg * J), 1)
-    head = lax.broadcasted_iota(jnp.int32, (wide, hg * J), 0)
-    for r in range(rpp):
-        for g in range(G):
-            hit = head == lane // J + (r * H + g * hg)
-            sel[r * G + g] = jnp.where(hit, 1.0, 0.0).astype(jnp.bfloat16)
+    lane = lax.broadcasted_iota(jnp.int32, (hg * J, wide), 1)
+    head = lax.broadcasted_iota(jnp.int32, (hg * J, wide), 0) // J
+    sel[...] = jnp.where(lax.rem(lane, hg) == head, 1.0, 0.0).astype(jnp.bfloat16)
 
     @pl.when(jnp.logical_not(last))
     def _():
         pl.semaphore_wait(ready, m)
 
-    for peer in second + third + peers.inside() + peers.at(peers.one):
+    other = peers.inside() + peers.at(peers.one)
+    for peer in near[:early] + far + near[early:] + other:
         u_copy(peer, me).start()
-    early = len(first)
-    for k, peer in enumerate(second):
-        if k < early:
-            @pl.when(inner)
-            def _(peer=peer):
-                k_copy(peer, me).start()
-        else:
-            k_copy(peer, me).start()
-    for k, peer in enumerate(third):
-        if k < early:
-            @pl.when(jnp.logical_not(inner))
-            def _(peer=peer):
-                k_copy(peer, me).start()
-        else:
-            k_copy(peer, me).start()
-    for peer in peers.inside() + peers.at(peers.one):
+    back = near[max(early, m - HELD) :]
+    for peer in far + near[early : max(early, m - HELD)] + other:
+        k_copy(peer, me).start()
+
+    for peer in back:
         k_copy(peer, me).start()
 
     rows = S * I
@@ -233,9 +231,8 @@
         for c in range(S):
             held = jnp.where(slot == c, stored[t, c], held)
             count = jnp.where(slot == c, sources[t, c], count)
-        spread[0, t] = held
-        spread[1, t] = count
-        spread[2, t] = (count * (J + 1) + lengths[t]) * T + t
+        owners[t : t + 1, :] = held
+        spread[t : t + 1, :] = count
 
     loads[2].wait()
     for g in range(G):
@@ -246,6 +243,15 @@
                 direct_r[h * D : (h + 1) * D].astype(jnp.float32).reshape(1, D), (rows, D)
             ).astype(jnp.bfloat16)
         ud[g] = dot_nt(states, rd[...])
+
+    held = owned[...]
+    target = lax.broadcasted_iota(jnp.int32, (T, S), 0)
+    target_counts = jnp.zeros((T, S), jnp.int32)
+    for t in range(T):
+        target_counts = jnp.where(target == t, lengths[t], target_counts)
+    codes = (owned_count[...] * (J + 1) + target_counts) * T + target
+    for v in range(C):
+        table[v] = jnp.max(jnp.where(held == v, codes, 0))
 
     token = lax.rem(lax.broadcasted_iota(jnp.int32, (1, rows), 1), I)
 
@@ -266,34 +272,48 @@
         tokens = total[:, 0:rows]
         for q in range(1, hg):
             tokens = tokens + total[:, q * rows : (q + 1) * rows]
-        count = spread[1, t]
-        dsum[t] = jnp.where(token < count, tokens, 0.0) / count.astype(jnp.float32)
+        count = spread[pl.ds(t, 1), :]
+        dsum[pl.ds(t, 1), :] = jnp.where(token < count, tokens, 0.0) / count.astype(jnp.float32)
         return carry
 
     lax.fori_loop(0, T, direct, 0)
 
     loads[3].wait()
     lanes = out.shape[1]
-    place = lax.broadcasted_iota(jnp.int32, (1, lanes), 1)
-    position = lax.rem(lax.broadcasted_iota(jnp.int32, (1, hg * J), 1), J)
     direct_sums = dsum[...]
-    owners = spread[0]
-    codes = spread[2]
+    owner = owners[...]
+    rows_of = wide // rpp
+    spot = lax.broadcasted_iota(jnp.int32, (T, wide), 1)
+    for p in range(n):
+        own = jnp.zeros((T, wide), jnp.float32)
+        for r in range(rpp):
+            part = jnp.where(owner == p * rpp + r, direct_sums, 0.0)
+            part = jnp.sum(part, axis=1, keepdims=True)
+            own = jnp.where(spot == r * rows_of, part, own)
+        owns[p] = own
+    RG = rpp * G
+    key = lax.broadcasted_iota(jnp.int32, (I, hg * J), 0)
+    row_of = lax.broadcasted_iota(jnp.int32, (RG, hg * J), 0) // G
+    position = lax.rem(lax.broadcasted_iota(jnp.int32, (RG, hg * J), 1), J)
+    row_of_sum = lax.broadcasted_iota(jnp.int32, (RG, wide), 0)
+    own_lanes = lax.broadcasted_iota(jnp.int32, (RG, wide), 1) // hg == row_of_sum
+    factor = math.log2(math.e) / math.sqrt(D)
 
     def lookup(p):
-        return [
-            jnp.max(jnp.where(owners == p * rpp + r, codes, 0)) for r in range(rpp)
-        ]
+        return [table[p * rpp + r] for r in range(rpp)]
 
     def block(p, found):
-        result = jnp.zeros((1, lanes), jnp.float32)
-        sent = u_buf[p]
+        limits = jnp.zeros((RG, hg * J), jnp.int32)
+        divisors = jnp.ones((RG, wide), jnp.float32)
         for r in range(rpp):
-            v = p * rpp + r
             t = lax.rem(found[r], T)
             target_count = lax.rem(found[r] // T, J + 1)
             source_count = found[r] // (T * (J + 1))
-            total = jnp.zeros((1, hg * J), jnp.float32)
+            limits = jnp.where(row_of == r, target_count, limits)
+            divisors = jnp.where(
+                row_of_sum // G == r, target_count.astype(jnp.float32), divisors
+            )
+            usable = key < source_count
             for g in range(G):
                 queries = jnp.concatenate(
                     [
@@ -303,17 +323,31 @@
                     axis=0,
                 )
                 scores = dot_nt(k_buf[p, r, :, g * D : (g + 1) * D], queries)
-                values = jnp.dot(
-                    sent, sel[r * G + g], preferred_element_type=jnp.float32
-                )
-                total = total + ratio(scores, values, source_count)
-            kept = jnp.where(position < target_count, total, 0.0)
-            channel = jnp.sum(kept, axis=1, keepdims=True)
-            channel = channel / target_count.astype(jnp.float32)
-            own = jnp.where(owners == v, direct_sums, 0.0)
-            own = jnp.sum(jnp.sum(own, axis=0), axis=1, keepdims=True)
-            result = result + jnp.where(place == me * rpp + r, own + channel, 0.0)
-        return result
+                scores = jnp.where(usable, scores, masked_score)
+                for c in range(0, hg * J, 128):
+                    score[c // 128, pl.ds(r * G + g, I, stride=RG), :] = scores[:, c : c + 128]
+        def at(k):
+            return jnp.concatenate(
+                [score[c, k * RG : (k + 1) * RG, :] for c in range(hg * J // 128)], axis=1
+            )
+        highest = at(0)
+        for k in range(1, I):
+            highest = jnp.maximum(highest, at(k))
+        weights = [jnp.exp2((at(k) - highest) * factor) for k in range(I)]
+        total = weights[0]
+        for k in range(1, I):
+            total = total + weights[k]
+        scale = jnp.where(position < limits, 1.0 / total, 0.0)
+        probs = jnp.concatenate(
+            [(w * scale).astype(jnp.bfloat16) for w in weights], axis=0
+        )
+        sums = jnp.dot(probs, sel[...], preferred_element_type=jnp.float32)
+        u = u_buf[p].astype(jnp.float32)
+        mixed = sums[0:RG] * u[0:1]
+        for k in range(1, I):
+            mixed = mixed + sums[k * RG : (k + 1) * RG] * u[k : k + 1]
+        mixed = jnp.where(own_lanes, mixed / divisors, 0.0)
+        return jnp.sum(mixed, axis=0, keepdims=True) + jnp.sum(owns[p], axis=0, keepdims=True)
 
     u_buf[me] = u_out[me]
     loads[1].wait()
@@ -326,20 +360,28 @@
         u_copy(p, p).wait_recv()
         r_out[p] = block(p, found)
         r_copy(p, me).start()
+
         return carry
 
     lax.fori_loop(0, n - 1, channel_step, 0)
 
-    def finish(i, carry):
-        p = peers.arrival(i)
-        r_copy(p, p).wait_recv()
-        k_copy(p, p).wait_send()
-        u_copy(p, p).wait_send()
-        r_copy(p, p).wait_send()
-        return carry
-
-    lax.fori_loop(0, n - 1, finish, 0)
-    out[...] = jnp.sum(r_buf[...], axis=0)
+    def settle(buffer, semaphore):
+        rest = buffer.at[pl.ds(0, n - 1)]
+        pltpu.make_async_copy(rest, rest, semaphore).wait()
+
+    settle(r_buf, rr)
+    settle(k_buf, ks)
+    settle(u_buf, us)
+    settle(r_buf, rs)
+    sums = r_buf[...].reshape(n, wide)
+    part = lax.broadcasted_iota(jnp.int32, (n, wide), 1) // rows_of
+    place = lax.broadcasted_iota(jnp.int32, (n, lanes), 1)
+    source = lax.broadcasted_iota(jnp.int32, (n, lanes), 0)
+    result = jnp.zeros((n, lanes), jnp.float32)
+    for r in range(rpp):
+        value = jnp.sum(jnp.where(part == r, sums, 0.0), axis=1, keepdims=True)
+        result = jnp.where(place == source * rpp + r, value, result)
+    out[...] = jnp.sum(result, axis=0, keepdims=True)
 
 
 def on_device(
@@ -379,6 +421,7 @@
             smem((T, S), jnp.int32),
             smem((T, S), jnp.int32),
             smem((T,), jnp.int32),
+            smem((C,), jnp.int32),
             vmem((QW,), bf),
             vmem((QW,), bf),
             vmem((T, S * I, QW), bf),
@@ -388,15 +431,20 @@
             vmem((n, rpp, I, G * HEAD_SIZE), bf),
             vmem((n, I, wide), bf),
             vmem((n, I, wide), bf),
-            vmem((3, T, 1, S * I), jnp.int32),
+            vmem((T, S * I), jnp.int32),
+            vmem((T, S * I), jnp.int32),
             vmem((G, T * J, hg * S * I), f32),
             vmem((hg * S * I, HEAD_SIZE), bf),
-            vmem((rpp * G, wide, hg * J), bf),
-            vmem((T, 1, S * I), f32),
-            vmem((n, 1, lanes), f32),
-            vmem((n, 1, lanes), f32),
-            dma((9,)), dma((T,)),
-            dma((n,)), dma((n,)), dma((n,)), dma((n,)), dma((n,)), dma((n,)),
+            vmem((hg * J, wide), bf),
+            vmem((hg * J // 128, I * rpp * G, 128), f32),
+            vmem((T, S), jnp.int32),
+            vmem((T, S), jnp.int32),
+            vmem((T, S * I), f32),
+            vmem((n, T, wide), f32),
+            vmem((n, 1, wide), f32),
+            vmem((n, 1, wide), f32),
+            dma((11,)), dma((T,)),
+            dma, dma((n,)), dma, dma((n,)), dma, dma,
             pltpu.SemaphoreType.REGULAR,
         ],
         compiler_params=pltpu.CompilerParams(

time: 36.8 us -> 35.9 us (0.976)
  the two profiles are of different devices: /device:TPU:1 before, /device:TPU:10 now
where the time goes in v2:
time: 35.9 us; the launch traced here: 35.7 us
  Pallas kernels  34.5 us (96%)
  local copies, waits for them, and re-layouts  1.19 us (3%)
    pallas_call x1, Pallas kernels, on_device(): pl.pallas_call(functools.partial(kernel, n, (T, S, I, J, H, G)), out_shap...  34.5 us
    squeeze x1, local copies, waits for them, and re-layouts, on_device(): return found[0, :C]  1.19 us

profile of v2, /device:TPU:10, one launch (start us, length us, event | category | flops | bytes accessed | tf_op | source)
XLA Modules:
  0.0 35.7 jit_solution(16980727918960902753)
XLA Ops:
  0.0 34.5 %shard_map.91 = f32[1,128]{1,0:T(1,128)} custom-call(s32[8,8]{1,0:T(8,128)} %stored_in.1, s32[8,8]{1,0:T(8,128)} %sources_in.1, s32[8]{0:T(128)} %lengths_in.1, bf16[4096]{0:T(1024)(128)(2,1)} %direct_in.1, bf16[4096]{0:T(1024)(128)(2,1)} %channel_in.1, bf16[8,128,4096]{2,1,0:T(8,128)(2,1)} %bitcast.4, bf16[8,32,1024]{2,1,0:T(8,128)(2,1)} %ts.1, ...), custom_call_target="tpu_custom_call" | custom-call | tf_op jit(solution)/shard_map/pallas_call | solution.py:412
  34.5 1.2 %slice_bitcast_fusion = f32[64]{0:T(128)} fusion(f32[1,128]{1,0:T(1,128)} %shard_map.91), kind=kLoop, calls=%fused_computation | loop fusion | bytes 512 | tf_op jit(solution)/shard_map/squeeze | solution.py:460

commit v3 on v2

--- a/solution.py
+++ b/solution.py
@@ -53,14 +53,17 @@
         i = i - (m - 1)
         early = lax.select(self.outer, 0, min(EARLY, m // 2))
         late = i - early
+        part = lax.div(lax.max(late, 0), m)
+        near = jnp.logical_or(late < 0, part == 2)
+        one = part == lax.select(self.outer, 1, 0)
+        j = lax.select(near, lax.select(late < 0, i, i - 2 * m), late - part * m)
+        back = jnp.logical_not(jnp.logical_or(self.outer, jnp.logical_and(one, late >= 0)))
+        j = lax.select(back, m - 1 - j, j)
+        base = lax.select(one, self.one, self.far)
+        base = lax.select(near, self.near, base)
         inside = i < 0
-        near = jnp.logical_or(i < early, i >= 2 * m + early)
-        j = lax.select(i < early, i, i - 2 * m)
-        j = lax.select(near, m - 1 - j, lax.rem(late + m, m))
+        base = lax.select(inside, self.me, base)
         j = lax.select(inside, i + m, j)
-        base = lax.select(late < m, self.far, self.one)
-        base = lax.select(near, self.near, base)
-        base = lax.select(inside, self.me, base)
         peer, bit = base, 1
         while bit < m:
             step = (1 - 2 * lax.rem(lax.div(self.me, bit), 2)) * bit

time: 35.9 us -> 34.5 us (0.961)
  Pallas kernels: 34.5 us -> 33.2 us
    pallas_call x1, Pallas kernels: 34.5 us -> 33.2 us  [on_device(): pl.pallas_call(functools.partial(kernel, n, (T, S, I, J, H, G)), out_shap...]
where the time goes in v3:
time: 34.5 us; the launch traced here: 34.4 us
  Pallas kernels  33.2 us (96%)
  local copies, waits for them, and re-layouts  1.19 us (3%)
    pallas_call x1, Pallas kernels, on_device(): pl.pallas_call(functools.partial(kernel, n, (T, S, I, J, H, G)), out_shap...  33.2 us
    squeeze x1, local copies, waits for them, and re-layouts, on_device(): return found[0, :C]  1.19 us

profile of v3, /device:TPU:10, one launch (start us, length us, event | category | flops | bytes accessed | tf_op | source)
XLA Modules:
  0.0 34.4 jit_solution(17304945798772180621)
XLA Ops:
  0.0 33.2 %shard_map.91 = f32[1,128]{1,0:T(1,128)} custom-call(s32[8,8]{1,0:T(8,128)} %stored_in.1, s32[8,8]{1,0:T(8,128)} %sources_in.1, s32[8]{0:T(128)} %lengths_in.1, bf16[4096]{0:T(1024)(128)(2,1)} %direct_in.1, bf16[4096]{0:T(1024)(128)(2,1)} %channel_in.1, bf16[8,128,4096]{2,1,0:T(8,128)(2,1)} %bitcast.4, bf16[8,32,1024]{2,1,0:T(8,128)(2,1)} %ts.1, ...), custom_call_target="tpu_custom_call" | custom-call | tf_op jit(solution)/shard_map/pallas_call | solution.py:415
  33.2 1.2 %slice_bitcast_fusion = f32[64]{0:T(128)} fusion(f32[1,128]{1,0:T(1,128)} %shard_map.91), kind=kLoop, calls=%fused_computation | loop fusion | bytes 512 | tf_op jit(solution)/shard_map/squeeze | solution.py:463

commit v4 on v3

--- a/solution.py
+++ b/solution.py
@@ -252,7 +252,8 @@
     target_counts = jnp.zeros((T, S), jnp.int32)
     for t in range(T):
         target_counts = jnp.where(target == t, lengths[t], target_counts)
-    codes = (owned_count[...] * (J + 1) + target_counts) * T + target
+    base, step = 1 << J.bit_length(), 1 << (T - 1).bit_length()
+    codes = (owned_count[...] * base + target_counts) * step + target
     for v in range(C):
         table[v] = jnp.max(jnp.where(held == v, codes, 0))
 
@@ -303,19 +304,23 @@
     factor = math.log2(math.e) / math.sqrt(D)
 
     def lookup(p):
-        return [table[p * rpp + r] for r in range(rpp)]
+        targets, counts = [], []
+        limits = jnp.zeros((RG, hg * J), jnp.int32)
+        for r in range(rpp):
+            code = table[p * rpp + r]
+            targets.append(lax.rem(code, step))
+            counts.append(lax.div(code, base * step))
+            limits = jnp.where(row_of == r, lax.rem(lax.div(code, step), base), limits)
+        kept = position < limits
+        shares = jnp.where(own_lanes, 1.0 / limits[:, :wide].astype(jnp.float32), 0.0)
+        own = jnp.sum(owns[p], axis=0, keepdims=True)
+        return targets, counts, kept, shares, own
 
     def block(p, found):
-        limits = jnp.zeros((RG, hg * J), jnp.int32)
-        divisors = jnp.ones((RG, wide), jnp.float32)
+        targets, counts, kept, shares, own = found
         for r in range(rpp):
-            t = lax.rem(found[r], T)
-            target_count = lax.rem(found[r] // T, J + 1)
-            source_count = found[r] // (T * (J + 1))
-            limits = jnp.where(row_of == r, target_count, limits)
-            divisors = jnp.where(
-                row_of_sum // G == r, target_count.astype(jnp.float32), divisors
-            )
+            t = targets[r]
+            source_count = counts[r]
             usable = key < source_count
             for g in range(G):
                 queries = jnp.concatenate(
@@ -340,7 +345,7 @@
         total = weights[0]
         for k in range(1, I):
             total = total + weights[k]
-        scale = jnp.where(position < limits, 1.0 / total, 0.0)
+        scale = jnp.where(kept, 1.0 / total, 0.0)
         probs = jnp.concatenate(
             [(w * scale).astype(jnp.bfloat16) for w in weights], axis=0
         )
@@ -349,8 +354,7 @@
         mixed = sums[0:RG] * u[0:1]
         for k in range(1, I):
             mixed = mixed + sums[k * RG : (k + 1) * RG] * u[k : k + 1]
-        mixed = jnp.where(own_lanes, mixed / divisors, 0.0)
-        return jnp.sum(mixed, axis=0, keepdims=True) + jnp.sum(owns[p], axis=0, keepdims=True)
+        return jnp.sum(mixed * shares, axis=0, keepdims=True) + own
 
     u_buf[me] = u_out[me]
     loads[1].wait()
@@ -451,7 +455,7 @@
             pltpu.SemaphoreType.REGULAR,
         ],
         compiler_params=pltpu.CompilerParams(
-            collective_id=0, has_side_effects=True, vmem_limit_bytes=60 << 20
+            collective_id=0, has_side_effects=True, vmem_limit_bytes=56553472
         ),
     )(
         candidate_row, candidate_length, target_length,

time: 34.5 us -> 33.3 us (0.965)
  local copies, waits for them, and re-layouts: 1.19 us -> 0.51 us
  Pallas kernels: 33.2 us -> 32.6 us
    squeeze x1, local copies, waits for them, and re-layouts: 1.19 us -> 0.51 us  [on_device(): return found[0, :C]]
    pallas_call x1, Pallas kernels: 33.2 us -> 32.6 us  [on_device(): pl.pallas_call(functools.partial(kernel, n, (T, S, I, J, H, G)), out_shap...]
where the time goes in v4:
time: 33.3 us; the launch traced here: 33.1 us
  Pallas kernels  32.6 us (98%)
  local copies, waits for them, and re-layouts  0.51 us (2%)
    pallas_call x1, Pallas kernels, on_device(): pl.pallas_call(functools.partial(kernel, n, (T, S, I, J, H, G)), out_shap...  32.6 us

profile of v4, /device:TPU:10, one launch (start us, length us, event | category | flops | bytes accessed | tf_op | source)
XLA Modules:
  0.0 33.1 jit_solution(2952225556035539528)
XLA Ops:
  0.0 32.6 %shard_map.91 = f32[1,128]{1,0:T(1,128)S(1)} custom-call(s32[8,8]{1,0:T(8,128)} %stored_in.1, s32[8,8]{1,0:T(8,128)} %sources_in.1, s32[8]{0:T(128)} %lengths_in.1, bf16[4096]{0:T(1024)(128)(2,1)} %direct_in.1, bf16[4096]{0:T(1024)(128)(2,1)} %channel_in.1, bf16[8,128,4096]{2,1,0:T(8,128)(2,1)} %bitcast.4, bf16[8,32,1024]{2,1,0:T(8,128)(2,1)} %ts.1, ...), custom_call_target="tpu_custom_call" | custom-call | tf_op jit(solution)/shard_map/pallas_call | solution.py:419
  32.6 0.5 %slice_bitcast_fusion = f32[64]{0:T(128)} fusion(f32[1,128]{1,0:T(1,128)S(1)} %shard_map.91), kind=kLoop, calls=%fused_computation | loop fusion | bytes 512 | tf_op jit(solution)/shard_map/squeeze | solution.py:467

commit v5 on v4

--- a/solution.py
+++ b/solution.py
@@ -11,8 +11,6 @@
 HEAD_SIZE = 128
 AXIS = "dp"
 MESH = pl.DeviceIdType.MESH
-EARLY = 2
-HELD = 2
 masked_score = -1e30
 
 
@@ -24,7 +22,7 @@
 
 class Peers:
     def __init__(self, me, n):
-        assert n >= 4 and n & (n - 1) == 0
+        assert n >= 8 and n & (n - 1) == 0
         m = n // 4
         self.me, self.n, self.m = me, n, m
         self.quarter = lax.div(me, m)
@@ -42,6 +40,10 @@
             bit *= 2
         self.steps = steps
 
+    def place(self, k):
+        m = self.m
+        return m // 2 - 1 if k == 0 else m - k - (m // 2 - 1 + k) // m
+
     def inside(self):
         return [self.me + s for s in self.steps[1:]]
 
@@ -51,14 +53,15 @@
     def arrival(self, i):
         m = self.m
         i = i - (m - 1)
-        early = lax.select(self.outer, 0, min(EARLY, m // 2))
+        early = lax.select(self.outer, 0, 1)
         late = i - early
         part = lax.div(lax.max(late, 0), m)
         near = jnp.logical_or(late < 0, part == 2)
         one = part == lax.select(self.outer, 1, 0)
         j = lax.select(near, lax.select(late < 0, i, i - 2 * m), late - part * m)
-        back = jnp.logical_not(jnp.logical_or(self.outer, jnp.logical_and(one, late >= 0)))
-        j = lax.select(back, m - 1 - j, j)
+        one = jnp.logical_and(one, late >= 0)
+        back = lax.select(near, lax.select(j == 0, m // 2 - 1, m - j - lax.div(m // 2 - 1 + j, m)), m - 1 - j)
+        j = lax.select(jnp.logical_or(self.outer, one), j, back)
         base = lax.select(one, self.one, self.far)
         base = lax.select(near, self.near, base)
         inside = i < 0
@@ -126,13 +129,36 @@
             semaphore, inc=1, device_id={AXIS: peer}, device_id_type=MESH
         )
 
-    for peer in peers.inside():
-        say(peer, barrier)
+    opens = peers.quarter == 0
+    middle = jnp.logical_not(jnp.logical_or(opens, last))
     cross = peers.at(peers.two) + peers.at(peers.three)
 
-    @pl.when(jnp.logical_not(last))
-    def _():
-        for peer in cross + peers.at(peers.one):
+    half = m // 2
+    ahead = lax.rem(lax.div(me, half), 2) == 0
+    first = jnp.logical_and(middle, ahead)
+    second = jnp.logical_and(middle, jnp.logical_not(ahead))
+    across = [base + step for base in (peers.three, me) for step in peers.steps[half:]]
+
+    @pl.when(middle)
+    def _():
+        for peer in peers.at(peers.three)[:half] + peers.at(peers.one) + peers.at(peers.two):
+            say(peer, barrier)
+        for peer in peers.inside()[: half - 1]:
+            say(peer, barrier)
+
+    @pl.when(first)
+    def _():
+        for peer in across:
+            say(peer, barrier)
+
+    @pl.when(opens)
+    def _():
+        for peer in peers.at(peers.three):
+            say(peer, barrier)
+
+    @pl.when(jnp.logical_not(middle))
+    def _():
+        for peer in peers.inside():
             say(peer, barrier)
 
     for load in loads[4:]:
@@ -166,15 +192,33 @@
         for peer in cross + peers.at(peers.one):
             say(peer, ready)
 
-    @pl.when(jnp.logical_not(last))
+    @pl.when(opens)
     def _():
         pl.semaphore_wait(barrier, n - 1 - m)
-
-    early = min(EARLY, m // 2)
+        for peer in peers.at(peers.one) + peers.at(peers.two):
+            say(peer, ready)
+
+    @pl.when(first)
+    def _():
+        pl.semaphore_wait(barrier, m - 1)
+
+    @pl.when(second)
+    def _():
+        pl.semaphore_wait(barrier, 2 * m - 1)
+        for peer in across:
+            say(peer, ready)
+
     far = peers.at(peers.far)
-    near = peers.at(peers.near)[::-1]
-    for peer in near[:early]:
-        k_copy(peer, me).start()
+    near = [
+        peers.near + lax.select(peers.outer, peers.steps[m - 1 - k], peers.steps[peers.place(k)])
+        for k in range(m)
+    ]
+    k_copy(near[0], me).start()
+
+    @pl.when(peers.outer)
+    def _():
+        k_copy(near[1], me).start()
+
     loads[1].start()
     for t in range(1, T):
         cq_copy(t).start()
@@ -210,18 +254,29 @@
     head = lax.broadcasted_iota(jnp.int32, (hg * J, wide), 0) // J
     sel[...] = jnp.where(lax.rem(lane, hg) == head, 1.0, 0.0).astype(jnp.bfloat16)
 
-    @pl.when(jnp.logical_not(last))
+    @pl.when(opens)
     def _():
         pl.semaphore_wait(ready, m)
 
+    @pl.when(first)
+    def _():
+        pl.semaphore_wait(ready, 3 * m)
+
+    @pl.when(second)
+    def _():
+        pl.semaphore_wait(ready, 2 * m)
+
     other = peers.inside() + peers.at(peers.one)
-    for peer in near[:early] + far + near[early:] + other:
+    for peer in near[:2] + far + near[2:] + other:
         u_copy(peer, me).start()
-    back = near[max(early, m - HELD) :]
-    for peer in far + near[early : max(early, m - HELD)] + other:
+    for peer in far:
         k_copy(peer, me).start()
 
-    for peer in back:
+    @pl.when(jnp.logical_not(peers.outer))
+    def _():
+        k_copy(near[1], me).start()
+
+    for peer in near[2:] + other:
         k_copy(peer, me).start()
 
     rows = S * I
@@ -283,7 +338,7 @@
     lax.fori_loop(0, T, direct, 0)
 
     loads[3].wait()
-    lanes = out.shape[1]
+    lanes = out.shape[0]
     direct_sums = dsum[...]
     owner = owners[...]
     rows_of = wide // rpp
@@ -388,7 +443,7 @@
     for r in range(rpp):
         value = jnp.sum(jnp.where(part == r, sums, 0.0), axis=1, keepdims=True)
         result = jnp.where(place == source * rpp + r, value, result)
-    out[...] = jnp.sum(result, axis=0, keepdims=True)
+    out[...] = jnp.sum(result, axis=0)
 
 
 def on_device(
@@ -418,7 +473,7 @@
     dma = pltpu.SemaphoreType.DMA
     found = pl.pallas_call(
         functools.partial(kernel, n, (T, S, I, J, H, G)),
-        out_shape=jax.ShapeDtypeStruct((1, lanes), f32),
+        out_shape=jax.ShapeDtypeStruct((C,), f32),
         in_specs=[
             anywhere, anywhere, anywhere, anywhere, anywhere,
             anywhere, anywhere, anywhere, anywhere,
@@ -464,7 +519,7 @@
         target_states, target_queries,
         candidate_states.reshape(n, rpp, I, 2 * G * HEAD_SIZE),
     )
-    return found[0, :C]
+    return found
 
 
 def solution(mesh):

time: 33.3 us -> 32.9 us (0.988)
    squeeze x1 -> x0, local copies, waits for them, and re-layouts: 0.51 us -> none  [on_device(): return found[0, :C]]
    unnamed x0 -> x1, local copies, waits for them, and re-layouts: none -> 0.51 us
    pallas_call x1, Pallas kernels: 32.6 us -> 32.3 us  [on_device(): pl.pallas_call(functools.partial(kernel, n, (T, S, I, J, H, G)), out_shap...]
where the time goes in v5:
time: 32.9 us; the launch traced here: 32.8 us
  Pallas kernels  32.3 us (98%)
  local copies, waits for them, and re-layouts  0.51 us (2%)
    pallas_call x1, Pallas kernels, on_device(): pl.pallas_call(functools.partial(kernel, n, (T, S, I, J, H, G)), out_shap...  32.3 us

profile of v5, /device:TPU:10, one launch (start us, length us, event | category | flops | bytes accessed | tf_op | source)
XLA Modules:
  0.0 32.8 jit_solution(3997994000370178803)
XLA Ops:
  0.0 32.3 %shard_map.91 = f32[64]{0:T(128)S(1)} custom-call(s32[8,8]{1,0:T(8,128)} %stored_in.1, s32[8,8]{1,0:T(8,128)} %sources_in.1, s32[8]{0:T(128)} %lengths_in.1, bf16[4096]{0:T(1024)(128)(2,1)} %direct_in.1, bf16[4096]{0:T(1024)(128)(2,1)} %channel_in.1, bf16[8,128,4096]{2,1,0:T(8,128)(2,1)} %bitcast.2, bf16[8,32,1024]{2,1,0:T(8,128)(2,1)} %ts.1, ...), custom_call_target="tpu_custom_call" | custom-call | tf_op jit(solution)/shard_map/pallas_call | solution.py:474
  32.3 0.5 %copy.11 = f32[64]{0:T(128)} copy(f32[64]{0:T(128)S(1)} %shard_map.91) | data formatting | bytes 512

commit v6 on v5

--- a/solution.py
+++ b/solution.py
@@ -92,7 +92,7 @@
     out,
     stored, sources, lengths, table, direct_r, channel_r,
     cq_buf, ts_buf, tq_buf, v_buf, k_buf, u_out, u_buf, spread, owners, ud, rd, sel, score, owned, owned_count, dsum, owns, r_out, r_buf,
-    in_sem, cq_sem, ks, kr, us, ur, rs, rr, ready,
+    in_sem, cq_sem, ks, kr, us, rs, rr, ready, both,
 ):
     T, S, I, J, H, G = dims
     C = T * S
@@ -177,7 +177,7 @@
     def u_copy(p, slot):
         return pltpu.make_async_remote_copy(
             src_ref=u_out.at[p], dst_ref=u_buf.at[slot], send_sem=us,
-            recv_sem=ur.at[slot], device_id={AXIS: p}, device_id_type=MESH,
+            recv_sem=kr.at[slot], device_id={AXIS: p}, device_id_type=MESH,
         )
 
     def r_copy(p, slot):
@@ -418,8 +418,7 @@
     def channel_step(i, carry):
         p = peers.arrival(i)
         found = lookup(p)
-        k_copy(p, p).wait_recv()
-        u_copy(p, p).wait_recv()
+        pltpu.make_async_copy(both, both, kr.at[p]).wait()
         r_out[p] = block(p, found)
         r_copy(p, me).start()
 
@@ -506,8 +505,9 @@
             vmem((n, 1, wide), f32),
             vmem((n, 1, wide), f32),
             dma((11,)), dma((T,)),
-            dma, dma((n,)), dma, dma((n,)), dma, dma,
+            dma, dma((n,)), dma, dma, dma,
             pltpu.SemaphoreType.REGULAR,
+            vmem((rpp * I * G + I * wide // HEAD_SIZE, HEAD_SIZE), bf),
         ],
         compiler_params=pltpu.CompilerParams(
             collective_id=0, has_side_effects=True, vmem_limit_bytes=56553472

time: 32.9 us -> 32.8 us (level)
  no operation moved by 1% of the time
where the time goes in v6:
time: 32.8 us; the launch traced here: 32.6 us
  Pallas kernels  32.1 us (98%)
  local copies, waits for them, and re-layouts  0.51 us (2%)
    pallas_call x1, Pallas kernels, on_device(): pl.pallas_call(functools.partial(kernel, n, (T, S, I, J, H, G)), out_shap...  32.1 us

profile of v6, /device:TPU:10, one launch (start us, length us, event | category | flops | bytes accessed | tf_op | source)
XLA Modules:
  0.0 32.6 jit_solution(6584691688735772356)
XLA Ops:
  0.0 32.1 %shard_map.91 = f32[64]{0:T(128)S(1)} custom-call(s32[8,8]{1,0:T(8,128)} %stored_in.1, s32[8,8]{1,0:T(8,128)} %sources_in.1, s32[8]{0:T(128)} %lengths_in.1, bf16[4096]{0:T(1024)(128)(2,1)} %direct_in.1, bf16[4096]{0:T(1024)(128)(2,1)} %channel_in.1, bf16[8,128,4096]{2,1,0:T(8,128)(2,1)} %bitcast.2, bf16[8,32,1024]{2,1,0:T(8,128)(2,1)} %ts.1, ...), custom_call_target="tpu_custom_call" | custom-call | tf_op jit(solution)/shard_map/pallas_call | solution.py:473
  32.1 0.5 %copy.11 = f32[64]{0:T(128)} copy(f32[64]{0:T(128)S(1)} %shard_map.91) | data formatting | bytes 512
